TPU v7x, 32 devices: a whole 2x2x4 slice. The times are simulated.
32 devices in a mesh: grp: 2 (over y), smp: 4 (over x, core), row: 4 (over z).
Axes of the slice: x: 2, y: 2, z: 4, core: 2. Of those that a mesh axis runs over, the one named last changes fastest.
Arguments:
- positions: float32 [8, 3, 4096], P(('grp', 'smp'), None, 'row'), parts along dimension 0, may hold values from -60 to 60
- noise_draw: float32 [8, 3, 4096], P(('grp', 'smp'), None, 'row'), parts along dimension 0, may hold values from -6 to 6
- noise_level: float32 [8], P(('grp', 'smp')), parts along dimension 0, may hold values from 0.5 to 80
- atom_single: bfloat16 [8192, 128], P(('grp', 'row')), parts along dimension 0, may hold values from -6 to 6
- token_single: bfloat16 [1024, 768], P(('grp', 'row')), parts along dimension 0, may hold values from -6 to 6
- pair_cond: bfloat16 [1024, 512, 128], P(('grp', 'row'), 'smp'), parts along dimension 0, may hold values from -6 to 6
- atom_to_token: int32 [8192], P(('grp', 'row')), parts along dimension 0, may hold values from 0 to 511, as said below
- window_offsets: int32 [256], P(('grp', 'row')), parts along dimension 0, may hold values from -96 to 0
- atom_mask: int32 [8192], P('grp'), parts along dimension 0, may hold values 0 or 1
- token_mask: int32 [1024], P('grp'), parts along dimension 0, may hold values 0 or 1
- coord_in: float32 [3, 128], replicated, may hold values from -3.5 to 3.5
- atom_gain: float32 [2, 128], replicated, may hold values from 0.1 to 1.9
- atom_qkv: bfloat16 [2, 128, 384], replicated, may hold values from -1 to 1
- atom_proj: bfloat16 [2, 128, 128], replicated, may hold values from -0.5 to 0.5
- gather_in: bfloat16 [128, 768], replicated, may hold values from -0.5 to 0.5
- noise_embed: float32 [768], replicated, may hold values from -6 to 6
- pair_gain: float32 [128], replicated, may hold values from 0.1 to 1.9
- pair_heads: bfloat16 [128, 16], replicated, may hold values from -0.5 to 0.5
- token_gain: float32 [2, 768], replicated, may hold values from 0.1 to 1.9
- token_qkv: bfloat16 [768, 2304], replicated, may hold values from -1 to 1
- token_proj: bfloat16 [768, 768], replicated, may hold values from -0.21875 to 0.21875
- ffn_in: bfloat16 [768, 3072], replicated, may hold values from -0.21875 to 0.21875
- ffn_out: bfloat16 [1536, 768], replicated, may hold values from -0.15625 to 0.15625
- scatter_out: bfloat16 [768, 128], replicated, may hold values from -0.21875 to 0.21875
- out_gain: float32 [128], replicated, may hold values from 0.1 to 1.9
- coord_out: bfloat16 [3, 128], replicated, may hold values from -0.5 to 0.5
Outputs:
- token_out: bfloat16 [8, 512, 768], P(('grp', 'smp'), 'row'), parts along dimension 0
- direction: float32 [8, 3, 4096], P(('grp', 'smp'), None, 'row'), parts along dimension 0
There are 2 independent parts, one for each index of `grp`. A program takes and returns all parts, laid end to end along the dimension named above; an argument that names none is the same for every part. Nothing has to cross between parts.
Inputs may be any that keep to these rules, and one draw needn't show every extreme that they name: `atom_to_token`: never falls along the atoms; atoms k * 1024 to (k + 1) * 1024 - 1 belong to tokens k * 128 to (k + 1) * 128 - 1; some tokens have no atom.
All inputs are finite; a program needn't handle non-finite values.
Results may differ from a plain program's by a relative error of at most 0.013.
Values may be sent and summed in bfloat16 or wider, within the bound.
A program may use at most 128 MiB of HBM per device.

v0:
```python
import jax
import jax.numpy as jnp
from jax import lax
from jax.sharding import PartitionSpec as P

D = 768
HEADS = 16
FF = 1536
CA = 128
AHEADS = 4
WQ = 32
WK = 128
HALO = 96
sigma_data = 16.0
gamma_boost = 0.8
norm_eps = 1e-05
masked_score = -1e30
outside_score = -2e30


def with_halo(block, sides, width):
    for axis, dim in sides:
        count = lax.axis_size(axis)
        forward = [(i, i + 1) for i in range(count - 1)]
        backward = [(target, source) for source, target in forward]
        low = lax.ppermute(
            lax.slice_in_dim(block, block.shape[dim] - width, None, axis=dim), axis, forward
        )
        high = lax.ppermute(lax.slice_in_dim(block, 0, width, axis=dim), axis, backward)
        block = jnp.concatenate([low, block, high], axis=dim)
    return block


def layer_norm(values, norm_gain):
    average = jnp.mean(values, axis=-1, keepdims=True)
    centred = values - average
    variance = jnp.mean(centred * centred, axis=-1, keepdims=True)
    return centred * lax.rsqrt(variance + norm_eps) * norm_gain


def softmax_rows(scores):
    largest = jnp.max(scores, axis=-1, keepdims=True)
    exponent = jnp.exp(scores - largest)
    return exponent / jnp.sum(exponent, axis=-1, keepdims=True)


def pair_bias_of(pair_tile, pair_gain, pair_heads):
    normed = layer_norm(pair_tile.astype(jnp.float32), pair_gain).astype(jnp.bfloat16)
    return jnp.einsum("ijc,ch->hij", normed, pair_heads, preferred_element_type=jnp.float32).astype(
        jnp.bfloat16
    )


def block_spans(extended, block_count, span_blocks):
    tail_shape = extended.shape[1:]
    grouped = extended.reshape((block_count + span_blocks - 1, WQ) + tail_shape)
    pieces = [grouped[shift : shift + block_count] for shift in range(span_blocks)]
    return jnp.stack(pieces, axis=1).reshape((block_count, span_blocks * WQ) + tail_shape)


def window_attend(queries, windows, live, inside, w_out):
    block_count = queries.shape[0] // WQ
    head_size = CA // AHEADS
    span_rows = windows.shape[1]
    query_heads = queries.reshape(block_count, WQ, AHEADS, head_size)
    key_heads = windows[:, :, :CA].reshape(block_count, span_rows, AHEADS, head_size)
    value_heads = windows[:, :, CA:].reshape(block_count, span_rows, AHEADS, head_size)
    scores = jnp.einsum(
        "bqhd,bkhd->bhqk", query_heads, key_heads, preferred_element_type=jnp.float32
    ) / jnp.sqrt(jnp.float32(head_size))
    scores = jnp.where(live[:, None, None, :], scores, masked_score)
    scores = jnp.where(inside[:, None, None, :], scores, outside_score)
    weights = softmax_rows(scores).astype(jnp.bfloat16)
    mixed_heads = jnp.einsum(
        "bhqk,bkhd->bqhd", weights, value_heads, preferred_element_type=jnp.float32
    ).astype(jnp.bfloat16)
    return jnp.dot(
        mixed_heads.reshape(block_count * WQ, CA), w_out, preferred_element_type=jnp.float32
    )


def atom_block(atom_state, norm_gain, w_qkv, w_out, offsets, live_ext):
    row_count = atom_state.shape[0]
    normed = layer_norm(atom_state, norm_gain).astype(jnp.bfloat16)
    widened = with_halo(normed, (("row", 0),), HALO)
    projected = jnp.dot(widened, w_qkv, preferred_element_type=jnp.float32).astype(jnp.bfloat16)
    queries = projected[HALO : HALO + row_count, :CA]
    extended = projected[:, CA:]
    block_count = row_count // WQ
    span_blocks = (2 * HALO + WQ) // WQ
    windows = block_spans(extended, block_count, span_blocks)
    live = block_spans(live_ext, block_count, span_blocks) > 0
    relative = jnp.arange(span_blocks * WQ, dtype=jnp.int32)[None, :]
    first_key = offsets[:, None] + HALO
    inside = (relative >= first_key) & (relative < first_key + WK)
    return atom_state + window_attend(queries, windows, live, inside, w_out)


def per_device(
    positions,
    noise_draw,
    noise_level,
    atom_single,
    token_single,
    pair_cond,
    atom_to_token,
    window_offsets,
    atom_mask,
    token_mask,
    coord_in,
    atom_gain,
    atom_qkv,
    atom_proj,
    gather_in,
    noise_embed,
    pair_gain,
    pair_heads,
    token_gain,
    token_qkv,
    token_proj,
    ffn_in,
    ffn_out,
    scatter_out,
    out_gain,
    coord_out,
):
    row_index = lax.axis_index("row")
    tok_rows = token_single.shape[0]
    atom_rows = atom_single.shape[0]
    head_size = D // HEADS
    biases = lax.all_gather(
        pair_bias_of(pair_cond, pair_gain, pair_heads), "smp", axis=2, tiled=True
    )
    local_token = atom_to_token - row_index * tok_rows
    valid_local = lax.dynamic_slice_in_dim(atom_mask, row_index * atom_rows, atom_rows)
    member = (local_token[None, :] == jnp.arange(tok_rows, dtype=jnp.int32)[:, None]) & (
        valid_local[None, :] > 0
    )
    onehot = member.astype(jnp.bfloat16)
    counts = jnp.maximum(jnp.sum(member.astype(jnp.float32), axis=1), 1.0)
    live_padded = jnp.pad(atom_mask, (HALO, HALO))
    live_ext = lax.dynamic_slice_in_dim(live_padded, row_index * atom_rows, atom_rows + 2 * HALO)
    key_live = token_mask > 0
    coords = positions[0]
    kicks = noise_draw[0]
    level_now = noise_level[0]
    level_hat = (1.0 + gamma_boost) * level_now
    noisy = coords + jnp.sqrt(level_hat * level_hat - level_now * level_now) * kicks
    scaled = noisy / jnp.sqrt(level_hat * level_hat + sigma_data * sigma_data)
    atom_state = atom_single.astype(jnp.float32) + jnp.einsum(
        "ka,kc->ac", scaled, coord_in, precision=lax.Precision.HIGHEST
    )
    atom_state = atom_block(
        atom_state, atom_gain[0], atom_qkv[0], atom_proj[0], window_offsets, live_ext
    )
    lifted = jax.nn.relu(
        jnp.dot(atom_state.astype(jnp.bfloat16), gather_in, preferred_element_type=jnp.float32)
    ).astype(jnp.bfloat16)
    pooled = jnp.dot(onehot, lifted, preferred_element_type=jnp.float32) / counts[:, None]
    token_state = (
        pooled
        + token_single.astype(jnp.float32)
        + jnp.log(level_hat / sigma_data) / 4.0 * noise_embed
    )
    normed = layer_norm(token_state, token_gain[0]).astype(jnp.bfloat16)
    projected = jnp.dot(normed, token_qkv, preferred_element_type=jnp.float32).astype(jnp.bfloat16)
    gathered = lax.all_gather(projected[:, D:], "row", axis=0, tiled=True)
    key_count = gathered.shape[0]
    query_heads = projected[:, :D].reshape(tok_rows, HEADS, head_size)
    key_heads = gathered[:, :D].reshape(key_count, HEADS, head_size)
    value_heads = gathered[:, D:].reshape(key_count, HEADS, head_size)
    scores = jnp.einsum(
        "ihd,jhd->hij", query_heads, key_heads, preferred_element_type=jnp.float32
    ) / jnp.sqrt(jnp.float32(head_size))
    scores = scores + biases.astype(jnp.float32)
    scores = jnp.where(key_live[None, None, :], scores, masked_score)
    weights = softmax_rows(scores).astype(jnp.bfloat16)
    mixed_heads = (
        jnp.einsum("hij,jhd->ihd", weights, value_heads, preferred_element_type=jnp.float32)
        .astype(jnp.bfloat16)
        .reshape(tok_rows, D)
    )
    token_state = token_state + jnp.dot(mixed_heads, token_proj, preferred_element_type=jnp.float32)
    normed = layer_norm(token_state, token_gain[1]).astype(jnp.bfloat16)
    hidden = jnp.dot(normed, ffn_in, preferred_element_type=jnp.float32)
    active = (jax.nn.silu(hidden[:, :FF]) * hidden[:, FF:]).astype(jnp.bfloat16)
    token_state = token_state + jnp.dot(active, ffn_out, preferred_element_type=jnp.float32)
    token_result = token_state.astype(jnp.bfloat16)
    spread_back = jnp.dot(token_result, scatter_out, preferred_element_type=jnp.float32).astype(
        jnp.bfloat16
    )
    atom_state = atom_state + lax.dot_general(
        onehot, spread_back, (((0,), (0,)), ((), ())), preferred_element_type=jnp.float32
    )
    atom_state = atom_block(
        atom_state, atom_gain[1], atom_qkv[1], atom_proj[1], window_offsets, live_ext
    )
    normed_out = layer_norm(atom_state, out_gain).astype(jnp.bfloat16)
    update = lax.dot_general(
        coord_out, normed_out, (((1,), (1,)), ((), ())), preferred_element_type=jnp.float32
    )
    base_square = sigma_data * sigma_data + level_hat * level_hat
    skip_scale = sigma_data * sigma_data / base_square
    out_scale = level_hat * sigma_data / jnp.sqrt(base_square)
    denoised = skip_scale * noisy + out_scale * update
    direction = (noisy - denoised) / level_hat
    return (token_result[None], direction[None])


def solution(mesh):
    in_specs = (
        P(("grp", "smp"), None, "row"),
        P(("grp", "smp"), None, "row"),
        P(("grp", "smp")),
        P(("grp", "row"), None),
        P(("grp", "row"), None),
        P(("grp", "row"), "smp", None),
        P(("grp", "row")),
        P(("grp", "row")),
        P("grp"),
        P("grp"),
        P(),
        P(),
        P(),
        P(),
        P(),
        P(),
        P(),
        P(),
        P(),
        P(),
        P(),
        P(),
        P(),
        P(),
        P(),
        P(),
    )
    out_specs = (P(("grp", "smp"), "row", None), P(("grp", "smp"), None, "row"))
    return jax.shard_map(
        per_device, mesh=mesh, in_specs=in_specs, out_specs=out_specs, check_vma=False
    )
```

profile of v0, /device:TPU:0, one launch (start us, length us, event | category | flops | bytes accessed | tf_op | source)
XLA Modules:
  0.0 203.9 jit_solution(14690072002025671553)
XLA Ops:
  13.7 5.6 %collective-permute-start = (bf16[96,128]{1,0:T(8,128)(2,1)}, bf16[96,128]{1,0:T(8,128)(2,1)}, u32[]{:S(2)}, u32[]{:S(2)}) collective-permute-start(bf16[96,128]{1,0:T(8,128)(2,1)} %get-tuple-element.32), channel_id=1, source_target_pairs={{0,1},{1,2},{2,3},{4,5},{5,6},{6,7},{8,9},{9,10},{10,11},{12,13},{... | collective-permute-start | bytes 73736 | tf_op jit(solution)/shard_map/ppermute | solution.py:26
  44.1 2.5 %fusion.117 = (bf16[32,224,128]{2,1,0:T(8,128)(2,1)}, bf16[32,224,128]{2,1,0:T(8,128)(2,1)}) fusion(bf16[32,224,256]{2,1,0:T(8,128)(2,1)S(1)} %bitcast.141), kind=kLoop, calls=%fused_computation.196 | loop fusion | bytes 7340032 | tf_op jit(solution)/shard_map/slice | solution.py:66
  46.5 4.0 %copy.78 = bf16[32,224,128]{1,2,0:T(8,128)(2,1)} copy(bf16[32,224,128]{2,1,0:T(8,128)(2,1)} %get-tuple-element.12) | data formatting | bytes 3670016 | tf_op jit(solution)/shard_map/slice | solution.py:66
  50.5 2.7 %reshape.297 = bf16[32,32,4,32]{3,2,1,0:T(4,128)(2,1)} reshape(bf16[1024,128]{1,0:T(8,128)(2,1)} %slice.290) | data formatting | bytes 524288 | tf_op jit(solution)/shard_map/reshape | solution.py:65
  53.3 3.9 %copy.77 = bf16[32,224,128]{1,2,0:T(8,128)(2,1)} copy(bf16[32,224,128]{2,1,0:T(8,128)(2,1)} %get-tuple-element.13) | data formatting | bytes 3670016 | tf_op jit(solution)/shard_map/slice | solution.py:67
  57.2 2.6 %fusion.49 = f32[32,4,32,224]{3,2,1,0:T(8,128)S(1)} fusion(bf16[32,224,4,32]{1,3,2,0:T(8,128)(2,1)} %bitcast.139, bf16[32,32,4,32]{3,2,1,0:T(4,128)(2,1)} %reshape.297), kind=kOutput, calls=%fused_computation.72 | convolution fusion | flops 58720256 | bytes 5767168 | tf_op jit(solution)/shard_map/bqhd,bkhd->bhqk/dot_general | solution.py:68
  59.9 6.4 %fusion.124 = (f32[32,4,32]{2,1,0:T(4,128)S(1)}, f32[32,4,32,224]{3,2,1,0:T(8,128)S(1)}) fusion(f32[32,4,32,224]{3,2,1,0:T(8,128)S(1)} %fusion.49, pred[32,224]{1,0:T(8,128)(4,1)S(1)} %copy-done.17, pred[32,224]{1,0:T(8,128)(4,1)S(1)} %copy-done.19), kind=kOutput, calls=%fused_computation.203 | output fusion | flops 7340255 | bytes 7370752 | tf_op jit(solution)/shard_map/sub | solution.py:43
  69.0 2.9 %reshape.299 = bf16[1024,128]{0,1:T(8,128)(2,1)} reshape(bf16[32,32,4,32]{1,0,3,2:T(8,128)(2,1)} %copy.80) | data formatting | bytes 524288 | tf_op jit(solution)/shard_map/reshape | solution.py:78
  74.1 3.3 %fusion.125 = (f32[128]{0:T(128)}, f32[128,768]{1,0:T(8,128)}) fusion(f32[768]{0:T(1024)} %broadcast_multiply_fusion.1, bf16[128,768]{1,0:T(8,128)(2,1)} %param.30, f32[128]{0:T(128)} %broadcast_maximum_fusion, bf16[128,768]{1,0:T(8,128)(2,1)} %param.40, f32[1024,128]{1,0:T(8,128)} %convolution_add_fusion.2, s32[1024]{0:T(1024)S(1)} %broadcast_subtract_fusion, ...), kind=kOutput, calls=%fused_computation.204 | convolution fusion | flops 405110656 | bytes 1319936 | tf_op jit(solution)/shard_map/dot_general | solution.py:159
  82.9 3.5 %convert_reduce_fusion = f32[128,128]{1,0:T(8,128)S(1)} fusion(bf16[128,128,128]{2,1,0:T(8,128)(2,1)} %param.31), kind=kLoop, calls=%fused_computation.4 | loop fusion | flops 4177920 | bytes 4259840 | tf_op jit(solution)/shard_map/reduce_sum | solution.py:35
  86.5 4.8 %fusion.5 = f32[128,128]{1,0:T(8,128)S(1)} fusion(bf16[128,128,128]{2,1,0:T(8,128)(2,1)S(1)} %copy-done.2, f32[128,128]{1,0:T(8,128)S(1)} %broadcast_multiply_fusion), kind=kLoop, calls=%fused_computation.7 | loop fusion | flops 8372224 | bytes 4325376 | tf_op jit(solution)/shard_map/reduce_sum | solution.py:37
  91.3 5.8 %fusion.8 = bf16[128,128,16]{1,2,0:T(8,128)(2,1)S(1)} fusion(bf16[128,128,128]{2,1,0:T(8,128)(2,1)S(1)} %copy-done.2, f32[128]{0:T(128)S(1)} %copy-done.27, f32[128,128]{1,0:T(8,128)S(1)} %add_rsqrt_fusion, f32[128,128]{1,0:T(8,128)S(1)} %broadcast_multiply_fusion, bf16[128,16]{0,1:T(8,128)(2,1)S(1)} %copy-done.25), kind=kOutput, calls=%fused_computation.10 | convolution fusion | flops 77594624 | bytes 4854272 | tf_op jit(solution)/shard_map/ijc,ch->hij/dot_general | solution.py:49
  98.4 23.7 %all-gather.3.cloned.1.call-done = bf16[512,1536]{1,0:T(8,128)(2,1)} async-done(((bf16[128,1536]{1,0:T(8,128)(2,1)}), bf16[512,1536]{1,0:T(8,128)(2,1)}) %all-gather.3.cloned.1.call-update) | async-done | bytes 1572880 | tf_op jit(solution)/shard_map/all_gather | solution.py:167
  124.1 21.2 %all-gather.5.cloned.1.call-done = bf16[16,128,512]{2,1,0:T(8,128)(2,1)} async-done(((bf16[16,128,128]{2,1,0:T(8,128)(2,1)}), bf16[16,128,512]{2,1,0:T(8,128)(2,1)}) %all-gather.5.cloned.1.call-update) | async-done | bytes 2097168 | tf_op jit(solution)/shard_map/all_gather | solution.py:131
  145.4 3.3 %fusion.128 = f32[16,128]{1,0:T(8,128)S(1)} fusion(bf16[16,128,512]{2,1,0:T(8,128)(2,1)} %all-gather.5.cloned.1.call-done, pred[512]{0:T(512)(128)(4,1)S(1)} %broadcast_compare_fusion.1, bf16[128,16,48]{0,2,1:T(8,128)(2,1)S(1)} %bitcast.165, bf16[512,16,48]{0,2,1:T(8,128)(2,1)S(1)} %bitcast.160), kind=kOutput, calls=%fused_computation.205 | convolution fusion | flops 106955264 | bytes 3088896 | tf_op jit(solution)/shard_map/sub | solution.py:43
  148.8 4.5 %fusion.40 = bf16[16,48,128]{2,1,0:T(8,128)(2,1)} fusion(bf16[512,16,48]{0,2,1:T(8,128)(2,1)S(1)} %bitcast.162, f32[16,128]{1,0:T(8,128)S(1)} %fusion.128, bf16[16,128,512]{2,1,0:T(8,128)(2,1)} %all-gather.5.cloned.1.call-done, pred[512]{0:T(512)(128)(4,1)} %copy-done.23, bf16[128,16,48]{0,2,1:T(8,128)(2,1)} %bitcast.166, bf16[512,16,48]{0,2,1:T(8,128)(2,1)S(1)} %bitcast.161), kind=kOutput, calls=%fused_computation.60 | convolution fusion | flops 208767488 | bytes 4071936 | tf_op jit(solution)/shard_map/hij,jhd->ihd/dot_general | solution.py:179
  154.9 3.3 %fusion.79 = f32[128,3072]{1,0:T(8,128)S(1)} fusion(bf16[768,3072]{1,0:T(8,128)(2,1)} %param.47, f32[128,768]{1,0:T(8,128)S(1)} %get-tuple-element.52, f32[768]{0:T(1024)S(1)} %get-tuple-element.8, f32[128]{0:T(128)S(1)} %add_rsqrt_fusion.4, f32[128]{0:T(128)S(1)} %broadcast_multiply_fusion.5), kind=kOutput, calls=%fused_computation.110 | convolution fusion | flops 604372992 | bytes 6688768 | tf_op jit(solution)/shard_map/dot_general | solution.py:185
  160.6 3.4 %collective-permute-start.2 = (bf16[96,128]{1,0:T(8,128)(2,1)S(1)}, bf16[96,128]{1,0:T(8,128)(2,1)S(1)}, u32[]{:S(2)}, u32[]{:S(2)}) collective-permute-start(bf16[96,128]{1,0:T(8,128)(2,1)S(1)} %get-tuple-element.30), channel_id=1, source_target_pairs={{0,1},{1,2},{2,3},{4,5},{5,6},{6,7},{8,9},{9,10},{10,11},{12,13},{... | collective-permute-start | bytes 73736 | tf_op jit(solution)/shard_map/ppermute | solution.py:26
  165.6 4.1 %collective-permute-done.3 = bf16[96,128]{1,0:T(8,128)(2,1)S(1)} collective-permute-done((bf16[96,128]{1,0:T(8,128)(2,1)S(1)}, bf16[96,128]{1,0:T(8,128)(2,1)S(1)}, u32[]{:S(2)}, u32[]{:S(2)}) %collective-permute-start.3) | collective-permute-done | bytes 24608 | tf_op jit(solution)/shard_map/ppermute | solution.py:29
  173.2 3.2 %copy.93 = bf16[32,224,128]{1,2,0:T(8,128)(2,1)S(1)} copy(bf16[32,224,128]{2,1,0:T(8,128)(2,1)} %get-tuple-element.10) | data formatting | bytes 3670016 | tf_op jit(solution)/shard_map/slice | solution.py:66
  177.5 4.3 %fusion.131 = (f32[32,4,32]{2,1,0:T(4,128)}, f32[32,4,32,224]{3,2,1,0:T(8,128)}) fusion(f32[32,4,32,224]{3,2,1,0:T(8,128)S(1)} %fusion.47, pred[32,224]{1,0:T(8,128)(4,1)S(1)} %copy-done.18, pred[32,224]{1,0:T(8,128)(4,1)S(1)} %copy-done.20), kind=kOutput, calls=%fused_computation.208 | output fusion | flops 7340255 | bytes 7370752 | tf_op jit(solution)/shard_map/sub | solution.py:43
  181.8 3.1 %copy.92 = bf16[32,224,128]{1,2,0:T(8,128)(2,1)} copy(bf16[32,224,128]{2,1,0:T(8,128)(2,1)S(1)} %copy-done.5) | data formatting | bytes 3670016 | tf_op jit(solution)/shard_map/slice | solution.py:67
  184.9 3.8 %fusion.36 = bf16[32,32,4,32]{1,3,2,0:T(8,128)(2,1)S(1)} fusion(bf16[32,224,4,32]{1,3,2,0:T(8,128)(2,1)} %bitcast.159, f32[32,4,32,224]{3,2,1,0:T(8,128)} %get-tuple-element.56, f32[32,4,32]{2,1,0:T(4,128)} %get-tuple-element.55), kind=kOutput, calls=%fused_computation.50 | convolution fusion | flops 60686336 | bytes 5783552 | tf_op jit(solution)/shard_map/bhqk,bkhd->bqhd/dot_general | solution.py:74
  190.4 2.9 %reshape.308 = bf16[1024,128]{0,1:T(8,128)(2,1)} reshape(bf16[32,32,4,32]{1,0,3,2:T(8,128)(2,1)} %copy.95) | data formatting | bytes 524288 | tf_op jit(solution)/shard_map/reshape | solution.py:78
  (150 shorter events, 59.1 us)
Async XLA Ops:
  7.2 72.2 %copy-start = (bf16[768,2304]{1,0:T(8,128)(2,1)S(1)}, bf16[768,2304]{1,0:T(8,128)(2,1)}, u32[]{:S(2)}) copy-start(bf16[768,2304]{1,0:T(8,128)(2,1)} %param.45) | copy-start | bytes 10616836
  7.2 114.9 %all-gather.3.cloned.1.call-start = ((), (), s32[]{:S(2)}) async-start(), calls=%async_computation | async-start | bytes 1966080 | tf_op jit(solution)/shard_map/all_gather | solution.py:167
  13.7 27.7 %collective-permute-start = (bf16[96,128]{1,0:T(8,128)(2,1)}, bf16[96,128]{1,0:T(8,128)(2,1)}, u32[]{:S(2)}, u32[]{:S(2)}) collective-permute-start(bf16[96,128]{1,0:T(8,128)(2,1)} %get-tuple-element.32), channel_id=1, source_target_pairs={{0,1},{1,2},{2,3},{4,5},{5,6},{6,7},{8,9},{9,10},{10,11},{12,13},{... | collective-permute-start | bytes 73736 | tf_op jit(solution)/shard_map/ppermute | solution.py:26
  19.3 22.1 %collective-permute-start.1 = (bf16[96,128]{1,0:T(8,128)(2,1)}, bf16[96,128]{1,0:T(8,128)(2,1)}, u32[]{:S(2)}, u32[]{:S(2)}) collective-permute-start(bf16[96,128]{1,0:T(8,128)(2,1)} %get-tuple-element.33), channel_id=1, source_target_pairs={{1,0},{2,1},{3,2},{5,4},{6,5},{7,6},{9,8},{10,9},{11,10},{13,12},{... | collective-permute-start | bytes 73736 | tf_op jit(solution)/shard_map/ppermute | solution.py:29
  59.9 6.4 %copy-start.8 = (bf16[32,224,128]{1,2,0:T(8,128)(2,1)S(1)}, bf16[32,224,128]{1,2,0:T(8,128)(2,1)}, u32[]{:S(2)}) copy-start(bf16[32,224,128]{1,2,0:T(8,128)(2,1)} %copy.77) | copy-start | bytes 5505028
  82.7 8.6 %copy-start.25 = (bf16[128,16]{0,1:T(8,128)(2,1)S(1)}, bf16[128,16]{0,1:T(8,128)(2,1)}, u32[]{:S(2)}) copy-start(bf16[128,16]{0,1:T(8,128)(2,1)} %param.43) | copy-start | bytes 12292
  82.7 8.6 %copy-start.27 = (f32[128]{0:T(128)S(1)}, f32[128]{0:T(128)}, u32[]{:S(2)}) copy-start(f32[128]{0:T(128)} %param.42) | copy-start | bytes 1540
  82.7 62.7 %all-gather.5.cloned.1.call-start = ((), (), s32[]{:S(2)}) async-start(), calls=%async_computation.1 | async-start | bytes 2621440 | tf_op jit(solution)/shard_map/all_gather | solution.py:131
  82.9 3.5 %copy-start.2 = (bf16[128,128,128]{2,1,0:T(8,128)(2,1)S(1)}, bf16[128,128,128]{2,1,0:T(8,128)(2,1)}, u32[]{:S(2)}) copy-start(bf16[128,128,128]{2,1,0:T(8,128)(2,1)} %param.31) | copy-start | bytes 12582916
  91.3 6.9 %copy-start.21 = (s32[512]{0:T(512)S(1)}, s32[512]{0:T(512)}, u32[]{:S(2)}) copy-start(s32[512]{0:T(512)} %param.35) | copy-start | bytes 6148
  91.3 6.9 %slice-start = ((bf16[128,2304]{1,0:T(8,128)(2,1)}), bf16[128,768]{1,0:T(8,128)(2,1)S(1)}, s32[]{:S(2)}) async-start(bf16[128,2304]{1,0:T(8,128)(2,1)} %copy-done.7), calls=%async_computation.2 | async-start | bytes 393216 | tf_op jit(solution)/shard_map/slice | solution.py:169
  98.2 50.6 %copy-start.23 = (pred[512]{0:T(512)(128)(4,1)}, pred[512]{0:T(512)(128)(4,1)S(1)}, u32[]{:S(2)}) copy-start(pred[512]{0:T(512)(128)(4,1)S(1)} %broadcast_compare_fusion.1) | copy-start | bytes 1540
  98.3 50.4 %copy-start.14 = (bf16[128,768]{0,1:T(8,128)(2,1)}, bf16[128,768]{0,1:T(8,128)(2,1)S(1)}, u32[]{:S(2)}) copy-start(bf16[128,768]{0,1:T(8,128)(2,1)S(1)} %copy.82) | copy-start | bytes 589828
  148.7 4.5 %copy-start.6 = (f32[128,768]{1,0:T(8,128)S(1)}, f32[128,768]{1,0:T(8,128)}, u32[]{:S(2)}) copy-start(f32[128,768]{1,0:T(8,128)} %get-tuple-element.50) | copy-start | bytes 1179652
  148.8 4.5 %copy-start.11 = (bf16[768,768]{1,0:T(8,128)(2,1)S(1)}, bf16[768,768]{1,0:T(8,128)(2,1)}, u32[]{:S(2)}) copy-start(bf16[768,768]{1,0:T(8,128)(2,1)} %param.46) | copy-start | bytes 3538948
  158.2 11.5 %copy-start.15 = (bf16[2,128,384]{2,1,0:T(8,128)(2,1)S(1)}, bf16[2,128,384]{2,1,0:T(8,128)(2,1)}, u32[]{:S(2)}) copy-start(bf16[2,128,384]{2,1,0:T(8,128)(2,1)} %param.38) | copy-start | bytes 589828
  159.3 10.8 %copy-start.13 = (bf16[128,768]{1,0:T(8,128)(2,1)}, bf16[128,768]{1,0:T(8,128)(2,1)S(1)}, u32[]{:S(2)}) copy-start(bf16[128,768]{1,0:T(8,128)(2,1)S(1)} %fusion.41) | copy-start | bytes 589828
  159.8 5.8 %copy-start.4 = (f32[1024,128]{1,0:T(8,128)}, f32[1024,128]{1,0:T(8,128)S(1)}, u32[]{:S(2)}) copy-start(f32[1024,128]{1,0:T(8,128)S(1)} %get-tuple-element.54) | copy-start | bytes 1572868
  160.6 5.0 %collective-permute-start.2 = (bf16[96,128]{1,0:T(8,128)(2,1)S(1)}, bf16[96,128]{1,0:T(8,128)(2,1)S(1)}, u32[]{:S(2)}, u32[]{:S(2)}) collective-permute-start(bf16[96,128]{1,0:T(8,128)(2,1)S(1)} %get-tuple-element.30), channel_id=1, source_target_pairs={{0,1},{1,2},{2,3},{4,5},{5,6},{6,7},{8,9},{9,10},{10,11},{12,13},{... | collective-permute-start | bytes 73736 | tf_op jit(solution)/shard_map/ppermute | solution.py:26
  164.0 5.7 %collective-permute-start.3 = (bf16[96,128]{1,0:T(8,128)(2,1)S(1)}, bf16[96,128]{1,0:T(8,128)(2,1)S(1)}, u32[]{:S(2)}, u32[]{:S(2)}) collective-permute-start(bf16[96,128]{1,0:T(8,128)(2,1)S(1)} %get-tuple-element.31), channel_id=1, source_target_pairs={{1,0},{2,1},{3,2},{5,4},{6,5},{7,6},{9,8},{10,9},{11,10},{13,12},{... | collective-permute-start | bytes 73736 | tf_op jit(solution)/shard_map/ppermute | solution.py:29
  177.5 4.3 %copy-start.5 = (bf16[32,224,128]{2,1,0:T(8,128)(2,1)S(1)}, bf16[32,224,128]{2,1,0:T(8,128)(2,1)}, u32[]{:S(2)}) copy-start(bf16[32,224,128]{2,1,0:T(8,128)(2,1)} %get-tuple-element.11) | copy-start | bytes 5505028
  184.9 12.2 %copy-start.1 = (bf16[768,2304]{1,0:T(8,128)(2,1)S(1)}, bf16[768,2304]{1,0:T(8,128)(2,1)}, u32[]{:S(2)}) copy-start(bf16[768,2304]{1,0:T(8,128)(2,1)} %param.45) | copy-start | bytes 10616836
  188.7 6.6 %copy-start.16 = (f32[1,3,1024]{2,0,1:T(1,128)S(1)}, f32[1,3,1024]{2,0,1:T(1,128)}, u32[]{:S(2)}) copy-start(f32[1,3,1024]{2,0,1:T(1,128)} %param.27) | copy-start | bytes 36868
  188.7 6.6 %copy-start.26 = (bf16[3,128]{1,0:T(4,128)(2,1)S(1)}, bf16[3,128]{1,0:T(4,128)(2,1)}, u32[]{:S(2)}) copy-start(bf16[3,128]{1,0:T(4,128)(2,1)} %param.51) | copy-start | bytes 2308
  (11 other events, 17.6 us)
Sparse Core Ops, SparseCore 0:
  82.8 39.2 all-gather.2
  123.7 21.6 all-gather.4
where the time goes:
time: 205 us; the launch traced here: 204 us
  local copies, waits for them, and re-layouts  56.3 us (27%)
  waiting for transfers between devices  49.1 us (24%)
  matrix products  41.6 us (20%)
  other arithmetic  29 us (14%)
  between operations  15.9 us (8%)
  starting transfers between devices  12 us (6%)
    all_gather x1, waiting for transfers between devices, per_device(): gathered = lax.all_gather(projected[:, D:], 'row', axis=0, tiled=True)  23.7 us
    all_gather x1, waiting for transfers between devices, per_device(): lax.all_gather(pair_bias_of(pair_cond, pair_gain, pair_heads), 'smp', axi...  21.2 us
    slice x4, local copies, waits for them, and re-layouts, window_attend(): windows[:, :, :CA].reshape(block_count, span_rows, AHEADS, head_size)  12.1 us
    sub x2, other arithmetic, softmax_rows(): exponent = jnp.exp(scores - largest)  10.7 us
    another operation x10, local copies, waits for them, and re-layouts, block_spans(): jnp.stack(pieces, axis=1)  10.6 us
    ppermute x2, starting transfers between devices, with_halo(): lax.ppermute(lax.slice_in_dim(block, block.shape[dim] - width, None, axis...  8.95 us
    reduce_sum x6, other arithmetic, layer_norm(): variance = jnp.mean(centred * centred, axis=-1, keepdims=True)  7.22 us
    slice x2, local copies, waits for them, and re-layouts, window_attend(): windows[:, :, CA:].reshape(block_count, span_rows, AHEADS, head_size)  7.01 us
  transfers between devices with their start and end apart: 6, of which 3 were waited for; matrix products, arithmetic and copies ran while one was open for 19% of the time, Pallas kernels for 0%

commit v1 on v0

--- a/solution.py
+++ b/solution.py
@@ -128,8 +128,8 @@
     tok_rows = token_single.shape[0]
     atom_rows = atom_single.shape[0]
     head_size = D // HEADS
-    biases = lax.all_gather(
-        pair_bias_of(pair_cond, pair_gain, pair_heads), "smp", axis=2, tiled=True
+    biases = jnp.concatenate(
+        lax.all_gather(pair_bias_of(pair_cond, pair_gain, pair_heads), "smp"), axis=2
     )
     local_token = atom_to_token - row_index * tok_rows
     valid_local = lax.dynamic_slice_in_dim(atom_mask, row_index * atom_rows, atom_rows)

time: 205 us -> 221 us (1.078)
  local copies, waits for them, and re-layouts: 56.3 us -> 67.3 us
  matrix products: 41.6 us -> 43.9 us
    convert_element_type x0 -> x2, local copies, waits for them, and re-layouts: none -> 10.1 us  [per_device(): scores = scores + biases.astype(jnp.float32)]
    sub x1 -> x0, matrix products: 3.33 us -> none  [softmax_rows(): exponent = jnp.exp(scores - largest)]
    dot_general x0 -> x1, matrix products: none -> 3.01 us  [per_device(): jnp.einsum('ihd,jhd->hij', query_heads, key_heads, preferred_element_type...]
    dot_general x1, matrix products: 4.49 us -> 7.3 us  [per_device(): jnp.einsum('hij,jhd->ihd', weights, value_heads, preferred_element_type=j...]
    unnamed x69 -> x67, local copies, waits for them, and re-layouts: 3.11 us -> 5.01 us
    sub x2 -> x3, other arithmetic: 10.7 us -> 12.4 us  [softmax_rows(): exponent = jnp.exp(scores - largest)]
  transfers between devices with their start and end apart: 6 -> 6, of which waited for: 3 -> 3; matrix products, arithmetic and copies ran while one was open for 19% -> 17% of each run, Pallas kernels for 0% -> 0%
where the time goes in v1:
time: 221 us; the launch traced here: 219 us
  local copies, waits for them, and re-layouts  67.3 us (30%)
  waiting for transfers between devices  49.4 us (22%)
  matrix products  43.9 us (20%)
  other arithmetic  31 us (14%)
  between operations  15.9 us (7%)
  starting transfers between devices  11.8 us (5%)
    all_gather x1, waiting for transfers between devices, per_device(): gathered = lax.all_gather(projected[:, D:], 'row', axis=0, tiled=True)  24.1 us
    all_gather x1, waiting for transfers between devices, per_device(): lax.all_gather(pair_bias_of(pair_cond, pair_gain, pair_heads), 'smp')  21.2 us
    sub x3, other arithmetic, softmax_rows(): exponent = jnp.exp(scores - largest)  12.4 us
    slice x4, local copies, waits for them, and re-layouts, window_attend(): windows[:, :, :CA].reshape(block_count, span_rows, AHEADS, head_size)  12.1 us
    another operation x10, local copies, waits for them, and re-layouts, block_spans(): jnp.stack(pieces, axis=1)  10.6 us
    convert_element_type x2, local copies, waits for them, and re-layouts, per_device(): scores = scores + biases.astype(jnp.float32)  10.1 us
    ppermute x2, starting transfers between devices, with_halo(): lax.ppermute(lax.slice_in_dim(block, block.shape[dim] - width, None, axis...  8.95 us
    reduce_sum x6, other arithmetic, layer_norm(): variance = jnp.mean(centred * centred, axis=-1, keepdims=True)  7.4 us
  transfers between devices with their start and end apart: 6, of which 3 were waited for; matrix products, arithmetic and copies ran while one was open for 17% of the time, Pallas kernels for 0%

profile of v1, /device:TPU:0, one launch (start us, length us, event | category | flops | bytes accessed | tf_op | source)
XLA Modules:
  0.0 219.2 jit_solution(6877878614388628958)
XLA Ops:
  13.7 5.6 %collective-permute-start = (bf16[96,128]{1,0:T(8,128)(2,1)}, bf16[96,128]{1,0:T(8,128)(2,1)}, u32[]{:S(2)}, u32[]{:S(2)}) collective-permute-start(bf16[96,128]{1,0:T(8,128)(2,1)} %get-tuple-element.32), channel_id=1, source_target_pairs={{0,1},{1,2},{2,3},{4,5},{5,6},{6,7},{8,9},{9,10},{10,11},{12,13},{... | collective-permute-start | bytes 73736 | tf_op jit(solution)/shard_map/ppermute | solution.py:26
  46.5 4.0 %copy.78 = bf16[32,224,128]{1,2,0:T(8,128)(2,1)} copy(bf16[32,224,128]{2,1,0:T(8,128)(2,1)} %get-tuple-element.12) | data formatting | bytes 3670016 | tf_op jit(solution)/shard_map/slice | solution.py:66
  50.5 2.7 %reshape.301 = bf16[32,32,4,32]{3,2,1,0:T(4,128)(2,1)} reshape(bf16[1024,128]{1,0:T(8,128)(2,1)} %slice.290) | data formatting | bytes 524288 | tf_op jit(solution)/shard_map/reshape | solution.py:65
  53.2 3.9 %copy.77 = bf16[32,224,128]{1,2,0:T(8,128)(2,1)} copy(bf16[32,224,128]{2,1,0:T(8,128)(2,1)} %get-tuple-element.13) | data formatting | bytes 3670016 | tf_op jit(solution)/shard_map/slice | solution.py:67
  59.8 6.4 %fusion.117 = (f32[32,4,32]{2,1,0:T(4,128)S(1)}, f32[32,4,32,224]{3,2,1,0:T(8,128)S(1)}) fusion(f32[32,4,32,224]{3,2,1,0:T(8,128)S(1)} %fusion.51, pred[32,224]{1,0:T(8,128)(4,1)S(1)} %copy-done.17, pred[32,224]{1,0:T(8,128)(4,1)S(1)} %copy-done.19), kind=kOutput, calls=%fused_computation.195 | output fusion | flops 7340255 | bytes 7370752 | tf_op jit(solution)/shard_map/sub | solution.py:43
  69.0 2.9 %reshape.303 = bf16[1024,128]{0,1:T(8,128)(2,1)} reshape(bf16[32,32,4,32]{1,0,3,2:T(8,128)(2,1)} %copy.80) | data formatting | bytes 524288 | tf_op jit(solution)/shard_map/reshape | solution.py:78
  74.2 3.4 %fusion.118 = (f32[128]{0:T(128)}, f32[128,768]{1,0:T(8,128)}) fusion(f32[768]{0:T(1024)} %broadcast_multiply_fusion.1, bf16[128,768]{1,0:T(8,128)(2,1)} %param.30, f32[128]{0:T(128)} %broadcast_maximum_fusion, bf16[128,768]{1,0:T(8,128)(2,1)} %param.40, f32[1024,128]{1,0:T(8,128)} %convolution_add_fusion.2, s32[1024]{0:T(1024)S(1)} %broadcast_subtract_fusion, ...), kind=kOutput, calls=%fused_computation.196 | convolution fusion | flops 405110656 | bytes 1319936 | tf_op jit(solution)/shard_map/dot_general | solution.py:159
  82.7 3.5 %convert_reduce_fusion = f32[128,128]{1,0:T(8,128)S(1)} fusion(bf16[128,128,128]{2,1,0:T(8,128)(2,1)} %param.31), kind=kLoop, calls=%fused_computation.4 | loop fusion | flops 4177920 | bytes 4259840 | tf_op jit(solution)/shard_map/reduce_sum | solution.py:35
  86.3 5.0 %fusion.5 = f32[128,128]{1,0:T(8,128)S(1)} fusion(bf16[128,128,128]{2,1,0:T(8,128)(2,1)S(1)} %copy-done.3, f32[128,128]{1,0:T(8,128)S(1)} %broadcast_multiply_fusion), kind=kLoop, calls=%fused_computation.7 | loop fusion | flops 8372224 | bytes 4325376 | tf_op jit(solution)/shard_map/reduce_sum | solution.py:37
  91.3 6.5 %fusion.36 = bf16[16,128,128]{2,0,1:T(8,128)(2,1)} fusion(bf16[128,128,128]{2,1,0:T(8,128)(2,1)S(1)} %copy-done.3, f32[128]{0:T(128)S(1)} %copy-done.26, f32[128,128]{1,0:T(8,128)S(1)} %add_rsqrt_fusion, f32[128,128]{1,0:T(8,128)S(1)} %broadcast_multiply_fusion, bf16[128,16]{0,1:T(8,128)(2,1)S(1)} %copy-done.24), kind=kOutput, calls=%fused_computation.49 | convolution fusion | flops 77856768 | bytes 4854272 | tf_op jit(solution)/shard_map/ijc,ch->hij/dot_general | solution.py:49
  98.0 24.1 %all-gather.4.cloned.1.call-done = bf16[512,1536]{1,0:T(8,128)(2,1)} async-done(((bf16[128,1536]{1,0:T(8,128)(2,1)}), bf16[512,1536]{1,0:T(8,128)(2,1)}) %all-gather.4.cloned.1.call-update) | async-done | bytes 1572880 | tf_op jit(solution)/shard_map/all_gather | solution.py:167
  124.1 21.2 %all-gather.6.cloned.1.call-done = bf16[64,128,128]{2,0,1:T(8,128)(2,1)} async-done(((bf16[16,128,128]{2,0,1:T(8,128)(2,1)}), bf16[64,128,128]{2,0,1:T(8,128)(2,1)}) %all-gather.6.cloned.1.call-update) | async-done | bytes 2097168 | tf_op jit(solution)/shard_map/all_gather | solution.py:132
  145.3 4.7 %copy.122 = f32[4,16,128,128]{3,0,2,1:T(4,128)} copy(bf16[4,16,128,128]{3,1,0,2:T(8,128)(2,1)} %bitcast.163) | data formatting | bytes 6291456 | tf_op jit(solution)/shard_map/convert_element_type | solution.py:175
  150.0 5.5 %reshape.313 = f32[16,128,512]{2,1,0:T(8,128)} reshape(f32[16,128,4,128]{3,2,1,0:T(4,128)} %bitcast.143) | data formatting | bytes 8388608 | tf_op jit(solution)/shard_map/convert_element_type | solution.py:175
  155.5 3.0 %add_select_fusion = f32[16,128,512]{2,1,0:T(8,128)S(1)} fusion(f32[16,128,512]{2,1,0:T(8,128)} %reshape.313, bf16[128,16,48]{0,2,1:T(8,128)(2,1)S(1)} %bitcast.167, bf16[512,16,48]{0,2,1:T(8,128)(2,1)S(1)} %bitcast.148, pred[512]{0:T(512)(128)(4,1)S(1)} %broadcast_compare_fusion.1), kind=kOutput, calls=%fused_computation.17 | convolution fusion | flops 103809024 | bytes 9372160 | tf_op jit(solution)/shard_map/ihd,jhd->hij/dot_general | solution.py:172
  162.2 7.3 %fusion.42 = bf16[16,48,128]{2,1,0:T(8,128)(2,1)S(1)} fusion(bf16[512,16,48]{0,2,1:T(8,128)(2,1)S(1)} %bitcast.166, f32[16,128]{1,0:T(8,128)S(1)} %fusion.121, f32[16,128,512]{2,1,0:T(8,128)} %copy-done.2), kind=kOutput, calls=%fused_computation.59 | convolution fusion | flops 103909888 | bytes 5185536 | tf_op jit(solution)/shard_map/hij,jhd->ihd/dot_general | solution.py:179
  170.2 3.3 %fusion.78 = f32[128,3072]{1,0:T(8,128)S(1)} fusion(bf16[768,3072]{1,0:T(8,128)(2,1)} %param.47, f32[128,768]{1,0:T(8,128)S(1)} %get-tuple-element.52, f32[768]{0:T(1024)S(1)} %get-tuple-element.8, f32[128]{0:T(128)S(1)} %add_rsqrt_fusion.4, f32[128]{0:T(128)S(1)} %broadcast_multiply_fusion.5), kind=kOutput, calls=%fused_computation.106 | convolution fusion | flops 604372992 | bytes 6688768 | tf_op jit(solution)/shard_map/dot_general | solution.py:185
  175.9 3.4 %collective-permute-start.2 = (bf16[96,128]{1,0:T(8,128)(2,1)S(1)}, bf16[96,128]{1,0:T(8,128)(2,1)S(1)}, u32[]{:S(2)}, u32[]{:S(2)}) collective-permute-start(bf16[96,128]{1,0:T(8,128)(2,1)S(1)} %get-tuple-element.30), channel_id=1, source_target_pairs={{0,1},{1,2},{2,3},{4,5},{5,6},{6,7},{8,9},{9,10},{10,11},{12,13},{... | collective-permute-start | bytes 73736 | tf_op jit(solution)/shard_map/ppermute | solution.py:26
  180.9 4.1 %collective-permute-done.3 = bf16[96,128]{1,0:T(8,128)(2,1)S(1)} collective-permute-done((bf16[96,128]{1,0:T(8,128)(2,1)S(1)}, bf16[96,128]{1,0:T(8,128)(2,1)S(1)}, u32[]{:S(2)}, u32[]{:S(2)}) %collective-permute-start.3) | collective-permute-done | bytes 24608 | tf_op jit(solution)/shard_map/ppermute | solution.py:29
  188.5 3.2 %copy.93 = bf16[32,224,128]{1,2,0:T(8,128)(2,1)S(1)} copy(bf16[32,224,128]{2,1,0:T(8,128)(2,1)} %get-tuple-element.10) | data formatting | bytes 3670016 | tf_op jit(solution)/shard_map/slice | solution.py:66
  192.8 4.3 %fusion.124 = (f32[32,4,32]{2,1,0:T(4,128)}, f32[32,4,32,224]{3,2,1,0:T(8,128)}) fusion(f32[32,4,32,224]{3,2,1,0:T(8,128)S(1)} %fusion.49, pred[32,224]{1,0:T(8,128)(4,1)S(1)} %copy-done.18, pred[32,224]{1,0:T(8,128)(4,1)S(1)} %copy-done.20), kind=kOutput, calls=%fused_computation.200 | output fusion | flops 7340255 | bytes 7370752 | tf_op jit(solution)/shard_map/sub | solution.py:43
  197.1 3.1 %copy.92 = bf16[32,224,128]{1,2,0:T(8,128)(2,1)} copy(bf16[32,224,128]{2,1,0:T(8,128)(2,1)S(1)} %copy-done.6) | data formatting | bytes 3670016 | tf_op jit(solution)/shard_map/slice | solution.py:67
  200.2 3.8 %fusion.32 = bf16[32,32,4,32]{1,3,2,0:T(8,128)(2,1)S(1)} fusion(bf16[32,224,4,32]{1,3,2,0:T(8,128)(2,1)} %bitcast.165, f32[32,4,32,224]{3,2,1,0:T(8,128)} %get-tuple-element.56, f32[32,4,32]{2,1,0:T(4,128)} %get-tuple-element.55), kind=kOutput, calls=%fused_computation.47 | convolution fusion | flops 60686336 | bytes 5783552 | tf_op jit(solution)/shard_map/bhqk,bkhd->bqhd/dot_general | solution.py:74
  205.7 2.9 %reshape.312 = bf16[1024,128]{0,1:T(8,128)(2,1)} reshape(bf16[32,32,4,32]{1,0,3,2:T(8,128)(2,1)} %copy.95) | data formatting | bytes 524288 | tf_op jit(solution)/shard_map/reshape | solution.py:78
  (150 shorter events, 65.7 us)
Async XLA Ops:
  7.2 72.2 %copy-start = (bf16[768,2304]{1,0:T(8,128)(2,1)S(1)}, bf16[768,2304]{1,0:T(8,128)(2,1)}, u32[]{:S(2)}) copy-start(bf16[768,2304]{1,0:T(8,128)(2,1)} %param.45) | copy-start | bytes 10616836
  7.2 114.9 %all-gather.4.cloned.1.call-start = ((), (), s32[]{:S(2)}) async-start(), calls=%async_computation | async-start | bytes 1966080 | tf_op jit(solution)/shard_map/all_gather | solution.py:167
  13.7 27.7 %collective-permute-start = (bf16[96,128]{1,0:T(8,128)(2,1)}, bf16[96,128]{1,0:T(8,128)(2,1)}, u32[]{:S(2)}, u32[]{:S(2)}) collective-permute-start(bf16[96,128]{1,0:T(8,128)(2,1)} %get-tuple-element.32), channel_id=1, source_target_pairs={{0,1},{1,2},{2,3},{4,5},{5,6},{6,7},{8,9},{9,10},{10,11},{12,13},{... | collective-permute-start | bytes 73736 | tf_op jit(solution)/shard_map/ppermute | solution.py:26
  19.2 22.1 %collective-permute-start.1 = (bf16[96,128]{1,0:T(8,128)(2,1)}, bf16[96,128]{1,0:T(8,128)(2,1)}, u32[]{:S(2)}, u32[]{:S(2)}) collective-permute-start(bf16[96,128]{1,0:T(8,128)(2,1)} %get-tuple-element.33), channel_id=1, source_target_pairs={{1,0},{2,1},{3,2},{5,4},{6,5},{7,6},{9,8},{10,9},{11,10},{13,12},{... | collective-permute-start | bytes 73736 | tf_op jit(solution)/shard_map/ppermute | solution.py:29
  57.2 2.6 %copy-start.19 = (pred[32,224]{1,0:T(8,128)(4,1)S(1)}, pred[32,224]{1,0:T(8,128)(4,1)}, u32[]{:S(2)}) copy-start(pred[32,224]{1,0:T(8,128)(4,1)} %fusion.93) | copy-start | bytes 21508
  59.8 6.4 %copy-start.9 = (bf16[32,224,128]{1,2,0:T(8,128)(2,1)S(1)}, bf16[32,224,128]{1,2,0:T(8,128)(2,1)}, u32[]{:S(2)}) copy-start(bf16[32,224,128]{1,2,0:T(8,128)(2,1)} %copy.77) | copy-start | bytes 5505028
  82.6 8.6 %copy-start.24 = (bf16[128,16]{0,1:T(8,128)(2,1)S(1)}, bf16[128,16]{0,1:T(8,128)(2,1)}, u32[]{:S(2)}) copy-start(bf16[128,16]{0,1:T(8,128)(2,1)} %param.43) | copy-start | bytes 12292
  82.7 8.6 %copy-start.26 = (f32[128]{0:T(128)S(1)}, f32[128]{0:T(128)}, u32[]{:S(2)}) copy-start(f32[128]{0:T(128)} %param.42) | copy-start | bytes 1540
  82.7 62.7 %all-gather.6.cloned.1.call-start = ((), (), s32[]{:S(2)}) async-start(), calls=%async_computation.1 | async-start | bytes 2621440 | tf_op jit(solution)/shard_map/all_gather | solution.py:132
  82.7 3.5 %copy-start.3 = (bf16[128,128,128]{2,1,0:T(8,128)(2,1)S(1)}, bf16[128,128,128]{2,1,0:T(8,128)(2,1)}, u32[]{:S(2)}) copy-start(bf16[128,128,128]{2,1,0:T(8,128)(2,1)} %param.31) | copy-start | bytes 12582916
  91.3 6.5 %copy-start.21 = (s32[512]{0:T(512)S(1)}, s32[512]{0:T(512)}, u32[]{:S(2)}) copy-start(s32[512]{0:T(512)} %param.35) | copy-start | bytes 6148
  91.3 6.5 %slice-start = ((bf16[128,2304]{1,0:T(8,128)(2,1)}), bf16[128,768]{1,0:T(8,128)(2,1)S(1)}, s32[]{:S(2)}) async-start(bf16[128,2304]{1,0:T(8,128)(2,1)} %copy-done.8), calls=%async_computation.2 | async-start | bytes 393216 | tf_op jit(solution)/shard_map/slice | solution.py:169
  162.1 7.3 %copy-start.7 = (f32[128,768]{1,0:T(8,128)S(1)}, f32[128,768]{1,0:T(8,128)}, u32[]{:S(2)}) copy-start(f32[128,768]{1,0:T(8,128)} %get-tuple-element.50) | copy-start | bytes 1179652
  162.2 7.3 %copy-start.12 = (bf16[768,768]{1,0:T(8,128)(2,1)S(1)}, bf16[768,768]{1,0:T(8,128)(2,1)}, u32[]{:S(2)}) copy-start(bf16[768,768]{1,0:T(8,128)(2,1)} %param.46) | copy-start | bytes 3538948
  169.9 3.5 %copy-start.23 = (bf16[1536,768]{1,0:T(8,128)(2,1)S(1)}, bf16[1536,768]{1,0:T(8,128)(2,1)}, u32[]{:S(2)}) copy-start(bf16[1536,768]{1,0:T(8,128)(2,1)} %param.48) | copy-start | bytes 7077892
  173.5 11.5 %copy-start.15 = (bf16[2,128,384]{2,1,0:T(8,128)(2,1)S(1)}, bf16[2,128,384]{2,1,0:T(8,128)(2,1)}, u32[]{:S(2)}) copy-start(bf16[2,128,384]{2,1,0:T(8,128)(2,1)} %param.38) | copy-start | bytes 589828
  174.6 10.8 %copy-start.14 = (bf16[128,768]{1,0:T(8,128)(2,1)}, bf16[128,768]{1,0:T(8,128)(2,1)S(1)}, u32[]{:S(2)}) copy-start(bf16[128,768]{1,0:T(8,128)(2,1)S(1)} %fusion.43) | copy-start | bytes 589828
  175.1 5.8 %copy-start.5 = (f32[1024,128]{1,0:T(8,128)}, f32[1024,128]{1,0:T(8,128)S(1)}, u32[]{:S(2)}) copy-start(f32[1024,128]{1,0:T(8,128)S(1)} %get-tuple-element.54) | copy-start | bytes 1572868
  175.9 5.0 %collective-permute-start.2 = (bf16[96,128]{1,0:T(8,128)(2,1)S(1)}, bf16[96,128]{1,0:T(8,128)(2,1)S(1)}, u32[]{:S(2)}, u32[]{:S(2)}) collective-permute-start(bf16[96,128]{1,0:T(8,128)(2,1)S(1)} %get-tuple-element.30), channel_id=1, source_target_pairs={{0,1},{1,2},{2,3},{4,5},{5,6},{6,7},{8,9},{9,10},{10,11},{12,13},{... | collective-permute-start | bytes 73736 | tf_op jit(solution)/shard_map/ppermute | solution.py:26
  179.3 5.7 %collective-permute-start.3 = (bf16[96,128]{1,0:T(8,128)(2,1)S(1)}, bf16[96,128]{1,0:T(8,128)(2,1)S(1)}, u32[]{:S(2)}, u32[]{:S(2)}) collective-permute-start(bf16[96,128]{1,0:T(8,128)(2,1)S(1)} %get-tuple-element.31), channel_id=1, source_target_pairs={{1,0},{2,1},{3,2},{5,4},{6,5},{7,6},{9,8},{10,9},{11,10},{13,12},{... | collective-permute-start | bytes 73736 | tf_op jit(solution)/shard_map/ppermute | solution.py:29
  192.8 4.3 %copy-start.6 = (bf16[32,224,128]{2,1,0:T(8,128)(2,1)S(1)}, bf16[32,224,128]{2,1,0:T(8,128)(2,1)}, u32[]{:S(2)}) copy-start(bf16[32,224,128]{2,1,0:T(8,128)(2,1)} %get-tuple-element.11) | copy-start | bytes 5505028
  200.2 12.2 %copy-start.1 = (bf16[768,2304]{1,0:T(8,128)(2,1)S(1)}, bf16[768,2304]{1,0:T(8,128)(2,1)}, u32[]{:S(2)}) copy-start(bf16[768,2304]{1,0:T(8,128)(2,1)} %param.45) | copy-start | bytes 10616836
  204.0 6.6 %copy-start.16 = (f32[1,3,1024]{2,0,1:T(1,128)S(1)}, f32[1,3,1024]{2,0,1:T(1,128)}, u32[]{:S(2)}) copy-start(f32[1,3,1024]{2,0,1:T(1,128)} %param.27) | copy-start | bytes 36868
  204.0 6.6 %copy-start.25 = (bf16[3,128]{1,0:T(4,128)(2,1)S(1)}, bf16[3,128]{1,0:T(4,128)(2,1)}, u32[]{:S(2)}) copy-start(bf16[3,128]{1,0:T(4,128)(2,1)} %param.51) | copy-start | bytes 2308
  (10 other events, 13.3 us)
Sparse Core Ops, SparseCore 0:
  82.8 39.2 all-gather.3
  123.6 21.6 all-gather.5
